TPU v7x, 256 devices: a whole 4x4x8 slice. The times are simulated.
256 devices in a mesh: dp: 64 (over y, z, core), tensor: 4 (over x).
Axes of the slice: x: 4, y: 4, z: 8, core: 2. Of those that a mesh axis runs over, the one named last changes fastest.
Arguments:
- hidden: bfloat16 [1024, 4096], P(('dp', 'tensor')), may hold values from -6 to 6
- shortcut: bfloat16 [1024, 4096], P('dp'), may hold values from -6 to 6
- expert_ids: int32 [1024, 2], P('dp'), may hold values from 0 to 7, all different within a row; in each aligned block of 16 rows (0 to 15, 16 to 31, ...) at most 6 rows name the same one
- route_weight: float32 [1024, 2], P('dp'), may hold values from 0.1 to 1
- dense_gain: float32 [4096], replicated, may hold values from 0.5 to 1.5
- moe_gain: float32 [4096], replicated, may hold values from 0.5 to 1.5
- dense_gate: bfloat16 [4096, 8192], P(None, 'dp'), may hold values from -0.09375 to 0.09375
- dense_lift: bfloat16 [4096, 8192], P(None, 'dp'), may hold values from -0.09375 to 0.09375
- dense_down: bfloat16 [8192, 4096], P('dp'), may hold values from -0.0625 to 0.0625
- expert_gate: bfloat16 [4096, 65536], P(None, ('dp', 'tensor')), may hold values from -0.09375 to 0.09375
- expert_lift: bfloat16 [4096, 65536], P(None, ('dp', 'tensor')), may hold values from -0.09375 to 0.09375
- expert_down: bfloat16 [65536, 4096], P(('dp', 'tensor')), may hold values from -0.0625 to 0.0625
Outputs:
- mixed: bfloat16 [1024, 4096], P(('dp', 'tensor'))
Inputs may be any that keep to these rules, and one draw needn't show every extreme that they name: `expert_ids`: the 2 experts of a token differ. In each aligned block of 16 rows (the tokens of one index of dp) no expert is named by more than 6 rows, and in every draw some expert is named by exactly 6 rows of some block; every expert is named somewhere.
All inputs are finite; a program needn't handle non-finite values.
Results may differ from a plain program's by a relative error of at most 0.006.
Values may be sent and summed in bfloat16 or wider, within the bound.
No kernel may reach another device: no remote copies, remote signals or barrier semaphores. Data moves between devices by JAX's collectives and lax.ppermute only.
A program may use at most 64 MiB of HBM per device.

v0:
```python
import jax
import jax.numpy as jnp
from jax import lax
from jax.sharding import PartitionSpec as P

D = 4096
E = 8
TOP = 2
CAP = 6
EPSILON = 1e-05


def cut_along(value, dim, devices):
    lengths = value.shape
    parts = value.reshape(*lengths[:dim], devices, lengths[dim] // devices, *lengths[dim + 1 :])
    return jnp.moveaxis(parts, dim, 0)


def summed_on_arrival(value, axis, dim):
    devices = lax.axis_size(axis)
    parts = lax.all_to_all(cut_along(value, dim, devices), axis, 0, 0, tiled=True)
    return jnp.sum(parts.astype(jnp.float32), axis=0)


def sent_and_summed(value, axis, dim):
    parts = cut_along(value, dim, lax.axis_size(axis))
    arrived = lax.all_to_all(parts, axis, split_axis=0, concat_axis=0, tiled=True)
    return arrived.sum(axis=0)


def normalize(values_in, gain):
    values = values_in.astype(jnp.float32)
    scale = lax.rsqrt(jnp.mean(values * values, axis=-1, keepdims=True) + EPSILON)
    return (values * scale * gain).astype(jnp.bfloat16)


def local(
    hidden,
    shortcut,
    expert_ids,
    route_weight,
    dense_gain,
    moe_gain,
    dense_gate,
    dense_lift,
    dense_down,
    expert_gate,
    expert_lift,
    expert_down,
):
    normed = normalize(hidden, dense_gain)
    piece = lax.all_gather(normed, "dp", axis=0, tiled=True)
    gate_vals = jnp.dot(piece, dense_gate, preferred_element_type=jnp.float32)
    lift_vals = jnp.dot(piece, dense_lift, preferred_element_type=jnp.float32)
    dense_inner = (jax.nn.silu(gate_vals) * lift_vals).astype(jnp.bfloat16)
    dense_out = summed_on_arrival(
        jnp.dot(dense_inner, dense_down, preferred_element_type=jnp.float32).astype(jnp.bfloat16),
        "dp",
        0,
    )
    members = lax.axis_size("dp") // E
    token_count = shortcut.shape[0]
    moe_in = normalize(shortcut, moe_gain)
    flat = expert_ids.reshape(token_count * TOP)
    picked = (flat[:, None] == jnp.arange(E, dtype=jnp.int32)[None, :]).astype(jnp.int32)
    before = jnp.cumsum(picked, axis=0) - picked
    places = flat * CAP + jnp.sum(before * picked, axis=1)
    chosen = (places[:, None] == jnp.arange(E * CAP, dtype=jnp.int32)[None, :]).astype(jnp.float32)
    chosen = chosen.reshape(token_count, TOP, E * CAP)
    spread = jnp.sum(chosen, axis=1).astype(jnp.bfloat16)
    weighted = jnp.sum(chosen * route_weight[:, :, None], axis=1)
    buffer = lax.dot_general(
        spread, moe_in, (((0,), (0,)), ((), ())), preferred_element_type=jnp.float32
    )
    buffer = buffer.astype(jnp.bfloat16).reshape(E, CAP, D)
    outgoing = jnp.repeat(buffer, members, axis=0)
    arrived = lax.all_to_all(outgoing, "dp", split_axis=0, concat_axis=0, tiled=True)
    sources, count, width = arrived.shape
    rows_in = arrived.reshape(sources * count, width)
    gate_vals = jnp.dot(rows_in, expert_gate, preferred_element_type=jnp.float32)
    lift_vals = jnp.dot(rows_in, expert_lift, preferred_element_type=jnp.float32)
    inner = (jax.nn.silu(gate_vals) * lift_vals).astype(jnp.bfloat16)
    terms = jnp.dot(inner, expert_down, preferred_element_type=jnp.float32).astype(jnp.bfloat16)
    returned = lax.all_to_all(
        terms.reshape(sources, count, D), "dp", split_axis=0, concat_axis=0, tiled=True
    )
    summed = jnp.sum(returned.astype(jnp.float32).reshape(E, members, CAP, D), axis=1).reshape(
        E * CAP, D
    )
    moe_part = jnp.dot(
        weighted, summed, precision=lax.Precision.HIGHEST, preferred_element_type=jnp.float32
    )
    moe_out = sent_and_summed(moe_part, "tensor", 0)
    return (hidden.astype(jnp.float32) + dense_out + moe_out).astype(jnp.bfloat16)


def solution(mesh):
    in_specs = (
        P(("dp", "tensor"), None),
        P("dp", None),
        P("dp", None),
        P("dp", None),
        P(),
        P(),
        P(None, "dp"),
        P(None, "dp"),
        P("dp", None),
        P(None, ("dp", "tensor")),
        P(None, ("dp", "tensor")),
        P(("dp", "tensor"), None),
    )
    out_specs = P(("dp", "tensor"), None)
    return jax.shard_map(local, mesh=mesh, in_specs=in_specs, out_specs=out_specs, check_vma=False)
```

profile of v0, /device:TPU:1, one launch (start us, length us, event | category | flops | bytes accessed | tf_op | source)
XLA Modules:
  0.0 332.7 jit_solution(13501166355664263416)
XLA Ops:
  6.5 0.9 copy.29
  8.7 1.0 fusion.7
  9.8 0.8 convert_reduce_fusion.2
  10.5 1.2 convolution_convert_fusion.2
  12.4 109.2 %all_to_all.20 = bf16[64,6,4096]{2,1,0:T(8,128)(2,1)} all-to-all(bf16[64,6,4096]{2,1,0:T(8,128)(2,1)S(1)} %bitcast.20), channel_id=1, replica_groups=mesh['dp'=64,'tensor'=4] {'dp'}, dimensions={0} | all-to-all | bytes 6291456 | tf_op jit(solution)/shard_map/all_to_all | solution.py:77
  121.6 5.7 %reshape.67 = bf16[384,4096]{1,0:T(8,128)(2,1)} reshape(bf16[64,6,4096]{2,1,0:T(8,128)(2,1)} %all_to_all.20) | data formatting | bytes 6291456 | tf_op jit(solution)/shard_map/reshape | solution.py:79
  127.3 3.5 %fusion.31 = f32[384,256]{1,0:T(8,128)S(1)} fusion(bf16[384,4096]{1,0:T(8,128)(2,1)} %reshape.67, bf16[4096,256]{1,0:T(8,128)(2,1)} %param.21), kind=kOutput, calls=%fused_computation.50 | convolution fusion | flops 805306368 | bytes 5636096 | tf_op jit(solution)/shard_map/dot_general | solution.py:80
  130.9 7.6 %convolution_convert_fusion = bf16[384,4096]{1,0:T(8,128)(2,1)} fusion(bf16[256,4096]{1,0:T(8,128)(2,1)S(1)} %copy-done, bf16[384,4096]{1,0:T(8,128)(2,1)} %reshape.67, bf16[4096,256]{1,0:T(8,128)(2,1)} %param.22, f32[384,256]{1,0:T(8,128)S(1)} %fusion.31), kind=kOutput, calls=%fused_computation.1 | convolution fusion | flops 1612775424 | bytes 10878976 | tf_op jit(solution)/shard_map/dot_general | solution.py:83
  138.5 5.6 %reshape.68 = bf16[64,6,4096]{2,1,0:T(8,128)(2,1)} reshape(bf16[384,4096]{1,0:T(8,128)(2,1)} %convolution_convert_fusion) | data formatting | bytes 6291456 | tf_op jit(solution)/shard_map/reshape | solution.py:85
  144.2 6.2 %all-to-all-start.2 = ((bf16[64,6,4096]{2,1,0:T(8,128)(2,1)}), bf16[64,6,4096]{2,1,0:T(8,128)(2,1)}, u32[]{:S(2)}, u32[]{:S(2)}) async-start(bf16[64,6,4096]{2,1,0:T(8,128)(2,1)} %reshape.68), calls=%async_computation.2 | async-start | bytes 8388608 | tf_op jit(solution)/shard_map/all_to_all | solution.py:84
  150.5 0.7 fusion.25
  151.3 90.5 %all-gather.3.cloned.1.call-done = bf16[64,4,4096]{2,1,0:T(4,128)(2,1)} async-done(((bf16[1,4,4096]{2,1,0:T(4,128)(2,1)}), bf16[64,4,4096]{2,1,0:T(4,128)(2,1)}) %all-gather.3.cloned.1.call-update) | async-done | bytes 2097168 | tf_op jit(solution)/shard_map/all_gather | solution.py:52
  241.7 4.0 %reshape.75 = bf16[256,4096]{1,0:T(8,128)(2,1)} reshape(bf16[64,4,4096]{2,1,0:T(4,128)(2,1)} %all-gather.3.cloned.1.call-done) | data formatting | bytes 4194304
  245.7 2.3 fusion.30
  248.0 4.8 %convolution_convert_fusion.1 = bf16[256,4096]{1,0:T(8,128)(2,1)} fusion(bf16[128,4096]{1,0:T(8,128)(2,1)} %param.20, bf16[256,4096]{1,0:T(8,128)(2,1)} %reshape.75, bf16[4096,128]{1,0:T(8,128)(2,1)} %param.19, f32[256,128]{1,0:T(8,128)S(1)} %fusion.30), kind=kOutput, calls=%fused_computation.2 | convolution fusion | flops 538116096 | bytes 6422528 | tf_op jit(solution)/shard_map/dot_general | solution.py:57
  252.8 4.1 %reshape.64 = bf16[64,4,4096]{2,1,0:T(4,128)(2,1)} reshape(bf16[256,4096]{1,0:T(8,128)(2,1)} %convolution_convert_fusion.1) | data formatting | bytes 4194304 | tf_op jit(solution)/shard_map/reshape | solution.py:15
  257.0 7.4 %all-to-all-start = ((bf16[64,4,4096]{2,1,0:T(4,128)(2,1)}), bf16[64,4,4096]{2,1,0:T(4,128)(2,1)}, u32[]{:S(2)}, u32[]{:S(2)}) async-start(bf16[64,4,4096]{2,1,0:T(4,128)(2,1)} %reshape.64), calls=%async_computation | async-start | bytes 4194304 | tf_op jit(solution)/shard_map/all_to_all | solution.py:21
  264.4 3.3 convert_reduce_fusion
  267.6 1.0 reshape.76
  268.6 2.4 fusion.32
  271.0 44.5 %all-to-all-done = bf16[64,4,4096]{2,1,0:T(4,128)(2,1)} async-done(((bf16[64,4,4096]{2,1,0:T(4,128)(2,1)}), bf16[64,4,4096]{2,1,0:T(4,128)(2,1)}, u32[]{:S(2)}, u32[]{:S(2)}) %all-to-all-start) | async-done | bytes 2097184 | tf_op jit(solution)/shard_map/all_to_all | solution.py:21
  315.5 3.9 %all-to-all-start.3 = ((f32[4,4,4096]{2,1,0:T(4,128)}), f32[4,4,4096]{2,1,0:T(4,128)S(1)}, u32[]{:S(2)}, u32[]{:S(2)}) async-start(f32[4,4,4096]{2,1,0:T(4,128)} %fusion.32), calls=%async_computation.3 | async-start | bytes 524288 | tf_op jit(solution)/shard_map/all_to_all | solution.py:27
  319.4 2.4 convert_reduce_fusion.1
  321.8 3.3 %all-to-all-done.3 = f32[4,4,4096]{2,1,0:T(4,128)S(1)} async-done(((f32[4,4,4096]{2,1,0:T(4,128)}), f32[4,4,4096]{2,1,0:T(4,128)S(1)}, u32[]{:S(2)}, u32[]{:S(2)}) %all-to-all-start.3) | async-done | bytes 262176 | tf_op jit(solution)/shard_map/all_to_all | solution.py:27
  (25 shorter events, 2.8 us)
Async XLA Ops:
  6.5 124.3 %copy-start = (bf16[256,4096]{1,0:T(8,128)(2,1)S(1)}, bf16[256,4096]{1,0:T(8,128)(2,1)}, u32[]{:S(2)}) copy-start(bf16[256,4096]{1,0:T(8,128)(2,1)} %param.23) | copy-start | bytes 6291460
  144.2 6.2 %copy-start.2 = (bf16[4,4096]{1,0:T(4,128)(2,1)S(1)}, bf16[4,4096]{1,0:T(4,128)(2,1)}, u32[]{:S(2)}) copy-start(bf16[4,4096]{1,0:T(4,128)(2,1)} %param.12) | copy-start | bytes 98308
  144.2 6.4 %copy-start.3 = (f32[4096]{0:T(1024)S(1)}, f32[4096]{0:T(1024)}, u32[]{:S(2)}) copy-start(f32[4096]{0:T(1024)} %param.16) | copy-start | bytes 49156
  144.2 112.8 %all-to-all-start.2 = ((bf16[64,6,4096]{2,1,0:T(8,128)(2,1)}), bf16[64,6,4096]{2,1,0:T(8,128)(2,1)}, u32[]{:S(2)}, u32[]{:S(2)}) async-start(bf16[64,6,4096]{2,1,0:T(8,128)(2,1)} %reshape.68), calls=%async_computation.2 | async-start | bytes 8388608 | tf_op jit(solution)/shard_map/all_to_all | solution.py:84
  150.3 91.4 %all-gather.3.cloned.1.call-start = ((), (), s32[]{:S(2)}) async-start(), calls=%async_computation.4 | async-start | bytes 2129920 | tf_op jit(solution)/shard_map/all_gather | solution.py:52
  151.3 94.5 %copy-start.1 = (bf16[4096,128]{1,0:T(8,128)(2,1)S(1)}, bf16[4096,128]{1,0:T(8,128)(2,1)}, u32[]{:S(2)}) copy-start(bf16[4096,128]{1,0:T(8,128)(2,1)} %param.18) | copy-start | bytes 3145732
  257.0 58.5 %all-to-all-start = ((bf16[64,4,4096]{2,1,0:T(4,128)(2,1)}), bf16[64,4,4096]{2,1,0:T(4,128)(2,1)}, u32[]{:S(2)}, u32[]{:S(2)}) async-start(bf16[64,4,4096]{2,1,0:T(4,128)(2,1)} %reshape.64), calls=%async_computation | async-start | bytes 4194304 | tf_op jit(solution)/shard_map/all_to_all | solution.py:21
  315.5 9.7 %all-to-all-start.3 = ((f32[4,4,4096]{2,1,0:T(4,128)}), f32[4,4,4096]{2,1,0:T(4,128)S(1)}, u32[]{:S(2)}, u32[]{:S(2)}) async-start(f32[4,4,4096]{2,1,0:T(4,128)} %fusion.32), calls=%async_computation.3 | async-start | bytes 524288 | tf_op jit(solution)/shard_map/all_to_all | solution.py:27
Sparse Core Ops, SparseCore 0:
  153.9 87.7 all-gather.2
where the time goes:
time: 334 us; the launch traced here: 333 us
  waiting for transfers between devices  138 us (41%)
  blocking collectives  109 us (33%)
  local copies, waits for them, and re-layouts  22.3 us (7%)
  matrix products  21.8 us (7%)
  starting transfers between devices  17.5 us (5%)
  between operations  13.5 us (4%)
  other arithmetic  10.1 us (3%)
    all_to_all x1, blocking collectives, local(): lax.all_to_all(outgoing, 'dp', split_axis=0, concat_axis=0, tiled=True)  109 us
    all_gather x1, waiting for transfers between devices, local(): piece = lax.all_gather(normed, 'dp', axis=0, tiled=True)  90.5 us
    all_to_all x1, waiting for transfers between devices, summed_on_arrival(): lax.all_to_all(cut_along(value, dim, devices), axis, 0, 0, tiled=True)  44.5 us
    dot_general x1, matrix products, local(): jnp.dot(inner, expert_down, preferred_element_type=jnp.float32)  7.64 us
    all_to_all x1, starting transfers between devices, summed_on_arrival(): lax.all_to_all(cut_along(value, dim, devices), axis, 0, 0, tiled=True)  7.4 us
  transfers between devices with their start and end apart: 4, of which 3 were waited for; matrix products, arithmetic and copies ran while one was open for 8% of the time, Pallas kernels for 0%

commit v1 on v0

--- a/solution.py
+++ b/solution.py
@@ -8,6 +8,24 @@
 TOP = 2
 CAP = 6
 EPSILON = 1e-05
+
+
+def laid_out(blocks, dim):
+    blocks = jnp.moveaxis(blocks, 0, dim)
+    dims = blocks.shape
+    return blocks.reshape(*dims[:dim], dims[dim] * dims[dim + 1], *dims[dim + 2 :])
+
+
+def doubled(shard, axis):
+    size = lax.axis_size(axis)
+    pieces = shard[None]
+    for level in range(size.bit_length() - 1):
+        apart = 1 << level
+        received = lax.ppermute(pieces, axis, [(i, i ^ apart) for i in range(size)])
+        both = jnp.stack([pieces, received])
+        upper = lax.axis_index(axis) >> level & 1
+        pieces = jnp.where(upper == 0, both, both[::-1]).reshape(-1, *shard.shape)
+    return pieces
 
 
 def cut_along(value, dim, devices):
@@ -49,7 +67,7 @@
     expert_down,
 ):
     normed = normalize(hidden, dense_gain)
-    piece = lax.all_gather(normed, "dp", axis=0, tiled=True)
+    piece = laid_out(doubled(normed, "dp"), 0)
     gate_vals = jnp.dot(piece, dense_gate, preferred_element_type=jnp.float32)
     lift_vals = jnp.dot(piece, dense_lift, preferred_element_type=jnp.float32)
     dense_inner = (jax.nn.silu(gate_vals) * lift_vals).astype(jnp.bfloat16)

time: 334 us -> 340 us (1.018)
  blocking collectives: 109 us -> 0 us
  waiting for transfers between devices: 138 us -> 219 us
  starting transfers between devices: 17.5 us -> 56.5 us
  between operations: 13.5 us -> 0.2 us
  other arithmetic: 10.1 us -> 17 us
    ppermute x0 -> x6, waiting for transfers between devices: none -> 171 us  [doubled(): received = lax.ppermute(pieces, axis, [(i, i ^ apart) for i in range(size)])]
    all_to_all x1 -> x0, blocking collectives: 109 us -> none  [local(): lax.all_to_all(outgoing, 'dp', split_axis=0, concat_axis=0, tiled=True)]
    all_gather x1 -> x0, waiting for transfers between devices: 90.5 us -> none  [local(): piece = lax.all_gather(normed, 'dp', axis=0, tiled=True)]
    all_to_all x1, starting transfers between devices: 7.4 us -> 21.2 us  [summed_on_arrival(): lax.all_to_all(cut_along(value, dim, devices), axis, 0, 0, tiled=True)]
    all_to_all x0 -> x1, starting transfers between devices: none -> 13.5 us  [local(): lax.all_to_all(outgoing, 'dp', split_axis=0, concat_axis=0, tiled=True)]
    ppermute x0 -> x6, starting transfers between devices: none -> 11 us  [doubled(): received = lax.ppermute(pieces, axis, [(i, i ^ apart) for i in range(size)])]
    another operation x0 -> x8, other arithmetic: none -> 4.36 us  [doubled(): both = jnp.stack([pieces, received])]
    another operation x0 -> x1, local copies, waits for them, and re-layouts: none -> 4.09 us  [laid_out(): blocks.reshape(*dims[:dim], dims[dim] * dims[dim + 1], *dims[dim + 2:])]
  transfers between devices with their start and end apart: 4 -> 10, of which waited for: 3 -> 7; matrix products, arithmetic and copies ran while one was open for 8% -> 16% of each run, Pallas kernels for 0% -> 0%
where the time goes in v1:
time: 340 us; the launch traced here: 339 us
  waiting for transfers between devices  219 us (64%)
  starting transfers between devices  56.5 us (17%)
  local copies, waits for them, and re-layouts  24.4 us (7%)
  matrix products  21.8 us (6%)
  other arithmetic  17 us (5%)
    ppermute x6, waiting for transfers between devices, doubled(): received = lax.ppermute(pieces, axis, [(i, i ^ apart) for i in range(size)])  171 us
    all_to_all x1, waiting for transfers between devices, summed_on_arrival(): lax.all_to_all(cut_along(value, dim, devices), axis, 0, 0, tiled=True)  44.5 us
    all_to_all x1, starting transfers between devices, summed_on_arrival(): lax.all_to_all(cut_along(value, dim, devices), axis, 0, 0, tiled=True)  21.2 us
    all_to_all x1, starting transfers between devices, local(): lax.all_to_all(outgoing, 'dp', split_axis=0, concat_axis=0, tiled=True)  13.5 us
    ppermute x6, starting transfers between devices, doubled(): received = lax.ppermute(pieces, axis, [(i, i ^ apart) for i in range(size)])  11 us
    dot_general x1, matrix products, local(): jnp.dot(inner, expert_down, preferred_element_type=jnp.float32)  7.64 us
  transfers between devices with their start and end apart: 10, of which 7 were waited for; matrix products, arithmetic and copies ran while one was open for 16% of the time, Pallas kernels for 0%

profile of v1, /device:TPU:1, one launch (start us, length us, event | category | flops | bytes accessed | tf_op | source)
XLA Modules:
  0.0 338.6 jit_solution(5690022049367147002)
XLA Ops:
  5.4 2.5 broadcast_in_dim.5
  7.9 13.5 %all-to-all-start.1 = ((bf16[64,6,4096]{2,1,0:T(8,128)(2,1)}), bf16[64,6,4096]{2,1,0:T(8,128)(2,1)}, u32[]{:S(2)}, u32[]{:S(2)}) async-start(bf16[64,6,4096]{2,1,0:T(8,128)(2,1)} %bitcast.40), calls=%async_computation.1 | async-start | bytes 8388608 | tf_op jit(solution)/shard_map/all_to_all | solution.py:95
  24.5 89.9 %collective-permute-done.1 = bf16[2,4,4096]{2,1,0:T(4,128)(2,1)S(1)} collective-permute-done((bf16[2,4,4096]{2,1,0:T(4,128)(2,1)S(1)}, bf16[2,4,4096]{2,1,0:T(4,128)(2,1)S(1)}, u32[]{:S(2)}, u32[]{:S(2)}) %collective-permute-start.1) | collective-permute-done | bytes 65568 | tf_op jit(solution)/shard_map/ppermute | solution.py:24
  115.0 8.7 %collective-permute-done.2 = bf16[4,4,4096]{2,1,0:T(4,128)(2,1)S(1)} collective-permute-done((bf16[4,4,4096]{2,1,0:T(4,128)(2,1)S(1)}, bf16[4,4,4096]{2,1,0:T(4,128)(2,1)S(1)}, u32[]{:S(2)}, u32[]{:S(2)}) %collective-permute-start.2) | collective-permute-done | bytes 131104 | tf_op jit(solution)/shard_map/ppermute | solution.py:24
  124.0 4.3 %collective-permute-start.3 = (bf16[8,4,4096]{2,1,0:T(4,128)(2,1)S(1)}, bf16[8,4,4096]{2,1,0:T(4,128)(2,1)S(1)}, u32[]{:S(2)}, u32[]{:S(2)}) collective-permute-start(bf16[8,4,4096]{2,1,0:T(4,128)(2,1)S(1)} %bitcast.45), channel_id=1, source_target_pairs={{0,32},{4,36},{8,40},{12,44},{16,48},{20,52},{24,56},{28,60},{32,0... | collective-permute-start | bytes 786440 | tf_op jit(solution)/shard_map/ppermute | solution.py:24
  128.3 5.7 %reshape.87 = bf16[384,4096]{1,0:T(8,128)(2,1)} reshape(bf16[64,6,4096]{2,1,0:T(8,128)(2,1)} %all-to-all-done.1) | data formatting | bytes 6291456 | tf_op jit(solution)/shard_map/reshape | solution.py:97
  134.0 3.5 %fusion.34 = f32[384,256]{1,0:T(8,128)S(1)} fusion(bf16[384,4096]{1,0:T(8,128)(2,1)} %reshape.87, bf16[4096,256]{1,0:T(8,128)(2,1)} %param.21), kind=kOutput, calls=%fused_computation.65 | convolution fusion | flops 805306368 | bytes 5636096 | tf_op jit(solution)/shard_map/dot_general | solution.py:98
  137.6 7.6 %convolution_convert_fusion = bf16[384,4096]{1,0:T(8,128)(2,1)} fusion(bf16[256,4096]{1,0:T(8,128)(2,1)S(1)} %copy-done, bf16[384,4096]{1,0:T(8,128)(2,1)} %reshape.87, bf16[4096,256]{1,0:T(8,128)(2,1)} %param.22, f32[384,256]{1,0:T(8,128)S(1)} %fusion.34), kind=kOutput, calls=%fused_computation.1 | convolution fusion | flops 1612775424 | bytes 10878976 | tf_op jit(solution)/shard_map/dot_general | solution.py:101
  145.2 5.6 %reshape.88 = bf16[64,6,4096]{2,1,0:T(8,128)(2,1)} reshape(bf16[384,4096]{1,0:T(8,128)(2,1)} %convolution_convert_fusion) | data formatting | bytes 6291456 | tf_op jit(solution)/shard_map/reshape | solution.py:103
  150.9 6.8 %all-to-all-start.2 = ((bf16[64,6,4096]{2,1,0:T(8,128)(2,1)}), bf16[64,6,4096]{2,1,0:T(8,128)(2,1)}, u32[]{:S(2)}, u32[]{:S(2)}) async-start(bf16[64,6,4096]{2,1,0:T(8,128)(2,1)} %reshape.88), calls=%async_computation.2 | async-start | bytes 8388608 | tf_op jit(solution)/shard_map/all_to_all | solution.py:102
  159.9 28.8 %collective-permute-done.4 = bf16[16,4,4096]{2,1,0:T(4,128)(2,1)S(1)} collective-permute-done((bf16[16,4,4096]{2,1,0:T(4,128)(2,1)S(1)}, bf16[16,4,4096]{2,1,0:T(4,128)(2,1)S(1)}, u32[]{:S(2)}, u32[]{:S(2)}) %collective-permute-start.4) | collective-permute-done | bytes 524320 | tf_op jit(solution)/shard_map/ppermute | solution.py:24
  190.0 2.7 collective-permute-start.5
  192.7 42.6 %collective-permute-done.5 = bf16[32,4,4096]{2,1,0:T(4,128)(2,1)} collective-permute-done((bf16[32,4,4096]{2,1,0:T(4,128)(2,1)S(1)}, bf16[32,4,4096]{2,1,0:T(4,128)(2,1)}, u32[]{:S(2)}, u32[]{:S(2)}) %collective-permute-start.5) | collective-permute-done | bytes 1048608 | tf_op jit(solution)/shard_map/ppermute | solution.py:24
  235.3 2.8 pad_maximum_fusion
  240.5 4.1 %reshape_reshape.3 = bf16[256,4096]{1,0:T(8,128)(2,1)} reshape(bf16[2,32,4,4096]{3,2,1,0:T(4,128)(2,1)} %reverse_select_fusion) | data formatting | bytes 4194304 | tf_op jit(solution)/shard_map/reshape;reshape | solution.py:16
  246.8 4.8 %convolution_convert_fusion.1 = bf16[256,4096]{1,0:T(8,128)(2,1)} fusion(bf16[128,4096]{1,0:T(8,128)(2,1)} %param.20, bf16[256,4096]{1,0:T(8,128)(2,1)} %reshape_reshape.3, bf16[4096,128]{1,0:T(8,128)(2,1)} %param.19, f32[256,128]{1,0:T(8,128)S(1)} %fusion.33), kind=kOutput, calls=%fused_computation.2 | convolution fusion | flops 538116096 | bytes 6422528 | tf_op jit(solution)/shard_map/dot_general | solution.py:75
  251.6 4.1 %reshape.84 = bf16[64,4,4096]{2,1,0:T(4,128)(2,1)} reshape(bf16[256,4096]{1,0:T(8,128)(2,1)} %convolution_convert_fusion.1) | data formatting | bytes 4194304 | tf_op jit(solution)/shard_map/reshape | solution.py:33
  255.8 21.2 %all-to-all-start = ((bf16[64,4,4096]{2,1,0:T(4,128)(2,1)}), bf16[64,4,4096]{2,1,0:T(4,128)(2,1)}, u32[]{:S(2)}, u32[]{:S(2)}) async-start(bf16[64,4,4096]{2,1,0:T(4,128)(2,1)} %reshape.84), calls=%async_computation | async-start | bytes 4194304 | tf_op jit(solution)/shard_map/all_to_all | solution.py:39
  277.0 3.3 convert_reduce_fusion
  281.3 2.4 fusion.35
  283.6 44.5 %all-to-all-done = bf16[64,4,4096]{2,1,0:T(4,128)(2,1)} async-done(((bf16[64,4,4096]{2,1,0:T(4,128)(2,1)}), bf16[64,4,4096]{2,1,0:T(4,128)(2,1)}, u32[]{:S(2)}, u32[]{:S(2)}) %all-to-all-start) | async-done | bytes 2097184 | tf_op jit(solution)/shard_map/all_to_all | solution.py:39
  328.1 4.0 %all-to-all-start.3 = ((f32[4,4,4096]{2,1,0:T(4,128)}), f32[4,4,4096]{2,1,0:T(4,128)S(1)}, u32[]{:S(2)}, u32[]{:S(2)}) async-start(f32[4,4,4096]{2,1,0:T(4,128)} %fusion.35), calls=%async_computation.3 | async-start | bytes 524288 | tf_op jit(solution)/shard_map/all_to_all | solution.py:45
  332.1 2.4 convert_reduce_fusion.1
  334.6 3.3 all-to-all-done.3
  (47 shorter events, 19.2 us)
Async XLA Ops:
  0.0 137.6 %copy-start = (bf16[256,4096]{1,0:T(8,128)(2,1)S(1)}, bf16[256,4096]{1,0:T(8,128)(2,1)}, u32[]{:S(2)}) copy-start(bf16[256,4096]{1,0:T(8,128)(2,1)} %param.23) | copy-start | bytes 6291460
  7.8 13.5 %copy-start.2 = (bf16[4,4096]{1,0:T(4,128)(2,1)S(1)}, bf16[4,4096]{1,0:T(4,128)(2,1)}, u32[]{:S(2)}) copy-start(bf16[4,4096]{1,0:T(4,128)(2,1)} %param.12) | copy-start | bytes 98308
  7.8 13.6 %copy-start.3 = (f32[4096]{0:T(1024)S(1)}, f32[4096]{0:T(1024)}, u32[]{:S(2)}) copy-start(f32[4096]{0:T(1024)} %param.16) | copy-start | bytes 49156
  7.9 120.5 %all-to-all-start.1 = ((bf16[64,6,4096]{2,1,0:T(8,128)(2,1)}), bf16[64,6,4096]{2,1,0:T(8,128)(2,1)}, u32[]{:S(2)}, u32[]{:S(2)}) async-start(bf16[64,6,4096]{2,1,0:T(8,128)(2,1)} %bitcast.40), calls=%async_computation.1 | async-start | bytes 8388608 | tf_op jit(solution)/shard_map/all_to_all | solution.py:95
  21.6 1.5 collective-permute-start
  23.2 91.2 %collective-permute-start.1 = (bf16[2,4,4096]{2,1,0:T(4,128)(2,1)S(1)}, bf16[2,4,4096]{2,1,0:T(4,128)(2,1)S(1)}, u32[]{:S(2)}, u32[]{:S(2)}) collective-permute-start(bf16[2,4,4096]{2,1,0:T(4,128)(2,1)S(1)} %get-tuple-element.8), channel_id=1, source_target_pairs={{0,8},{4,12},{8,0},{12,4},{16,24},{20,28},{24,16},{28,20},{32,40},... | collective-permute-start | bytes 196616 | tf_op jit(solution)/shard_map/ppermute | solution.py:24
  114.5 9.2 %collective-permute-start.2 = (bf16[4,4,4096]{2,1,0:T(4,128)(2,1)S(1)}, bf16[4,4,4096]{2,1,0:T(4,128)(2,1)S(1)}, u32[]{:S(2)}, u32[]{:S(2)}) collective-permute-start(bf16[4,4,4096]{2,1,0:T(4,128)(2,1)S(1)} %bitcast.47), channel_id=1, source_target_pairs={{0,16},{4,20},{8,24},{12,28},{16,0},{20,4},{24,8},{28,12},{32,48},... | collective-permute-start | bytes 393224 | tf_op jit(solution)/shard_map/ppermute | solution.py:24
  124.0 33.6 %collective-permute-start.3 = (bf16[8,4,4096]{2,1,0:T(4,128)(2,1)S(1)}, bf16[8,4,4096]{2,1,0:T(4,128)(2,1)S(1)}, u32[]{:S(2)}, u32[]{:S(2)}) collective-permute-start(bf16[8,4,4096]{2,1,0:T(4,128)(2,1)S(1)} %bitcast.45), channel_id=1, source_target_pairs={{0,32},{4,36},{8,40},{12,44},{16,48},{20,52},{24,56},{28,60},{32,0... | collective-permute-start | bytes 786440 | tf_op jit(solution)/shard_map/ppermute | solution.py:24
  150.9 104.9 %all-to-all-start.2 = ((bf16[64,6,4096]{2,1,0:T(8,128)(2,1)}), bf16[64,6,4096]{2,1,0:T(8,128)(2,1)}, u32[]{:S(2)}, u32[]{:S(2)}) async-start(bf16[64,6,4096]{2,1,0:T(8,128)(2,1)} %reshape.88), calls=%async_computation.2 | async-start | bytes 8388608 | tf_op jit(solution)/shard_map/all_to_all | solution.py:102
  158.3 30.5 %collective-permute-start.4 = (bf16[16,4,4096]{2,1,0:T(4,128)(2,1)S(1)}, bf16[16,4,4096]{2,1,0:T(4,128)(2,1)S(1)}, u32[]{:S(2)}, u32[]{:S(2)}) collective-permute-start(bf16[16,4,4096]{2,1,0:T(4,128)(2,1)S(1)} %bitcast.43), channel_id=1, source_target_pairs={{0,64},{4,68},{8,72},{12,76},{16,80},{20,84},{24,88},{28,92},{32,9... | collective-permute-start | bytes 1572872 | tf_op jit(solution)/shard_map/ppermute | solution.py:24
  190.0 45.3 %collective-permute-start.5 = (bf16[32,4,4096]{2,1,0:T(4,128)(2,1)S(1)}, bf16[32,4,4096]{2,1,0:T(4,128)(2,1)}, u32[]{:S(2)}, u32[]{:S(2)}) collective-permute-start(bf16[32,4,4096]{2,1,0:T(4,128)(2,1)S(1)} %bitcast.41), channel_id=1, source_target_pairs={{0,128},{4,132},{8,136},{12,140},{16,144},{20,148},{24,152},{28,15... | collective-permute-start | bytes 3145736 | tf_op jit(solution)/shard_map/ppermute | solution.py:24
  240.5 4.1 %copy-start.1 = (bf16[4096,128]{1,0:T(8,128)(2,1)S(1)}, bf16[4096,128]{1,0:T(8,128)(2,1)}, u32[]{:S(2)}) copy-start(bf16[4096,128]{1,0:T(8,128)(2,1)} %param.18) | copy-start | bytes 3145732
  255.8 72.3 %all-to-all-start = ((bf16[64,4,4096]{2,1,0:T(4,128)(2,1)}), bf16[64,4,4096]{2,1,0:T(4,128)(2,1)}, u32[]{:S(2)}, u32[]{:S(2)}) async-start(bf16[64,4,4096]{2,1,0:T(4,128)(2,1)} %reshape.84), calls=%async_computation | async-start | bytes 4194304 | tf_op jit(solution)/shard_map/all_to_all | solution.py:39
  328.1 9.8 %all-to-all-start.3 = ((f32[4,4,4096]{2,1,0:T(4,128)}), f32[4,4,4096]{2,1,0:T(4,128)S(1)}, u32[]{:S(2)}, u32[]{:S(2)}) async-start(f32[4,4,4096]{2,1,0:T(4,128)} %fusion.35), calls=%async_computation.3 | async-start | bytes 524288 | tf_op jit(solution)/shard_map/all_to_all | solution.py:45
